TPU v7x, 32 devices: a whole 2x2x4 slice. The times are simulated.
32 devices in a mesh: rows: 4 (over x, core), cols: 8 (over z, y).
Axes of the slice: x: 2, y: 2, z: 4, core: 2. Of those that a mesh axis runs over, the one named last changes fastest.
Arguments:
- pair_integrals: float32 [4096, 4096], P('rows', 'cols'), may hold values from -6 to 6
- left_factor: float32 [4096, 1024], P('rows', 'cols'), may hold values from -0.9375 to 0.9375
- core: float32 [1024, 1024], replicated, may hold values from -6 to 6
- right_factor: float32 [4096, 1024], P('cols', 'rows'), may hold values from -0.9375 to 0.9375
Outputs:
- core_next: float32 [1024, 1024], replicated
All inputs are finite; a program needn't handle non-finite values.
Results may differ from a plain program's by a relative error of at most 0.000062.
Values sent between devices are 32-bit elements; how exact they have to be, the bound alone decides.
No kernel may reach another device: no remote copies, remote signals or barrier semaphores. Data moves between devices by JAX's collectives and lax.ppermute only.
A program may use at most 128 MiB of HBM per device.

v0:
```python
import jax
import jax.numpy as jnp
from jax import lax
from jax.sharding import PartitionSpec as P


def product(left, right):
    return jnp.dot(left, right, precision=lax.Precision.HIGHEST, preferred_element_type=jnp.float32)


def shards(pair_integrals, left_factor, core, right_factor):
    left_rows = lax.all_gather(left_factor, "cols", axis=1, tiled=True)
    right_rows = lax.all_gather(right_factor, "rows", axis=1, tiled=True)
    mixed = product(core, right_rows.T)
    residual = pair_integrals - product(left_rows, mixed)
    along = product(residual, right_rows)
    local_term = product(left_rows.T, along)
    gradient = lax.psum(local_term, ("rows", "cols"))
    numer = jnp.sum(gradient * gradient)
    image = product(left_rows, product(gradient, right_rows.T))
    denom = lax.psum(jnp.sum(image * image), ("rows", "cols"))
    return core + numer / denom * gradient


def solution(mesh):
    return jax.shard_map(
        shards,
        mesh=mesh,
        in_specs=(P("rows", "cols"), P("rows", "cols"), P(), P("cols", "rows")),
        out_specs=P(),
        check_vma=False,
    )
```

profile of v0, /device:TPU:0, one launch (start us, length us, event | category | flops | bytes accessed | tf_op | source)
XLA Modules:
  0.0 382.8 jit_solution(6131846957028007544)
XLA Ops:
  6.5 0.0 all-gather.3.cloned.1.call-start
  6.5 0.7 all-gather.3.cloned.1.call-update
  7.3 0.0 all-gather.5.cloned.1.call-start
  7.3 0.7 all-gather.5.cloned.1.call-update
  8.0 0.0 all-reduce.2.cloned.1.call-start
  8.1 26.2 %all-gather.3.cloned.1.call-done = f32[512,1024]{1,0:T(8,128)} async-done(((f32[512,256]{1,0:T(8,128)}), f32[512,1024]{1,0:T(8,128)}) %all-gather.3.cloned.1.call-update) | async-done | bytes 2097168 | tf_op jit(solution)/shard_map/all_gather | solution.py:13
  34.2 10.2 %fusion.1 = f32[1024,512]{1,0:T(8,128)} fusion(f32[1024,1024]{1,0:T(8,128)} %param.6, f32[512,1024]{1,0:T(8,128)} %all-gather.3.cloned.1.call-done), kind=kOutput, calls=%fused_computation.6 | convolution fusion | flops 6442450944 | bytes 8388608 | tf_op jit(solution)/shard_map/dot_general | solution.py:8
  44.5 0.0 copy-start
  44.5 66.5 %all-gather.5.cloned.1.call-done = f32[1024,1024]{1,0:T(8,128)} async-done(((f32[1024,128]{1,0:T(8,128)}), f32[1024,1024]{1,0:T(8,128)}) %all-gather.5.cloned.1.call-update) | async-done | bytes 4194320 | tf_op jit(solution)/shard_map/all_gather | solution.py:12
  110.9 0.0 copy-start.3
  110.9 10.0 %fusion.2 = f32[512,1024]{0,1:T(8,128)S(1)} fusion(f32[1024,512]{1,0:T(8,128)} %fusion.1, f32[1024,1024]{1,0:T(8,128)} %all-gather.5.cloned.1.call-done), kind=kOutput, calls=%fused_computation.7 | convolution fusion | flops 6442450944 | bytes 8388608 | tf_op jit(solution)/shard_map/dot_general | solution.py:8
  120.9 0.0 copy-done
  120.9 0.0 copy-done.3
  120.9 0.0 copy-start.1
  120.9 6.9 %fusion = f32[1024,1024]{1,0:T(8,128)S(1)} fusion(f32[512,1024]{1,0:T(8,128)S(1)} %copy-done, f32[1024,512]{1,0:T(8,128)S(1)} %copy-done.3, f32[512,1024]{0,1:T(8,128)S(1)} %fusion.2), kind=kOutput, calls=%fused_computation.4 | convolution fusion | flops 6442975232 | bytes 10485760 | tf_op jit(solution)/shard_map/dot_general | solution.py:8
  127.8 0.0 copy-done.1
  127.8 14.9 %convolution_bitcast_fusion = f32[1024,1024]{0,1:T(8,128)} fusion(f32[1024,1024]{1,0:T(8,128)S(1)} %fusion, f32[1024,1024]{1,0:T(8,128)S(1)} %copy-done.1), kind=kOutput, calls=%fused_computation.2 | convolution fusion | flops 12884901888 | bytes 12582912 | tf_op jit(solution)/shard_map/dot_general | solution.py:8
  142.7 0.0 all-reduce.2.cloned.1.call-update
  142.7 140.8 %all-reduce.2.cloned.1.call-done = f32[1024,1024]{0,1:T(8,128)} async-done(((f32[1024,1024]{0,1:T(8,128)}), f32[1024,1024]{0,1:T(8,128)}) %all-reduce.2.cloned.1.call-update) | async-done | bytes 4194320 | tf_op jit(solution)/shard_map/psum | solution.py:18
  283.5 0.0 copy-start.2
  283.5 15.6 %fusion.3 = f32[1024,512]{1,0:T(8,128)S(1)} fusion(f32[1024,1024]{0,1:T(8,128)} %all-reduce.2.cloned.1.call-done, f32[512,1024]{1,0:T(8,128)S(1)} %copy-done), kind=kOutput, calls=%fused_computation.8 | convolution fusion | flops 6442450944 | bytes 8388608 | tf_op jit(solution)/shard_map/dot_general | solution.py:8
  299.2 0.0 copy-done.2
  299.2 14.3 %multiply_reduce_fusion.1 = f32[]{:T(128)} fusion(f32[1024,512]{1,0:T(8,128)S(1)} %fusion.3, f32[1024,1024]{1,0:T(8,128)S(1)} %copy-done.2), kind=kOutput, calls=%fused_computation.5 | convolution fusion | flops 6443499520 | bytes 6291460 | tf_op jit(solution)/shard_map/dot_general | solution.py:8
  313.5 5.3 %copy.5 = f32[1024,1024]{0,1:T(8,128)} copy(f32[1024,1024]{1,0:T(8,128)} %param.6) | data formatting | bytes 8388608 | tf_op args[2]
  318.9 39.5 %psum.15 = f32[]{:T(128)} all-reduce(f32[]{:T(128)} %multiply_reduce_fusion.1), channel_id=1, replica_groups=mesh['rows'=4,'cols'=8] {'rows','cols'}, use_global_device_ids=true, to_apply=%region_3.0 | all-reduce | flops 1 | bytes 8 | tf_op jit(solution)/shard_map/psum | solution.py:21
  358.3 3.9 %multiply_reduce_fusion = f32[]{:T(128)} fusion(f32[1024,1024]{0,1:T(8,128)} %all-reduce.2.cloned.1.call-done), kind=kLoop, calls=%fused_computation.1 | loop fusion | flops 2097151 | bytes 4194308 | tf_op jit(solution)/shard_map/reduce_sum | solution.py:19
  363.6 6.9 %multiply_add_fusion = f32[1024,1024]{0,1:T(8,128)} fusion(f32[1024,1024]{0,1:T(8,128)} %copy.5, f32[1024,1024]{0,1:T(8,128)} %all-reduce.2.cloned.1.call-done, f32[]{:T(128)S(6)} %div.3), kind=kLoop, calls=%fused_computation | loop fusion | flops 2097152 | bytes 12582916 | tf_op jit(solution)/shard_map/add | solution.py:22
  370.4 5.3 %copy.6 = f32[1024,1024]{1,0:T(8,128)} copy(f32[1024,1024]{0,1:T(8,128)} %multiply_add_fusion) | data formatting | bytes 8388608 | tf_op jit(solution)/shard_map/add | solution.py:22
Async XLA Ops:
  6.5 27.7 %all-gather.3.cloned.1.call-start = ((), (), s32[]{:S(2)}) async-start(), calls=%async_computation | async-start | bytes 2621440 | tf_op jit(solution)/shard_map/all_gather | solution.py:13
  7.3 103.7 %all-gather.5.cloned.1.call-start = ((), (), s32[]{:S(2)}) async-start(), calls=%async_computation.1 | async-start | bytes 4718592 | tf_op jit(solution)/shard_map/all_gather | solution.py:12
  8.0 275.5 %all-reduce.2.cloned.1.call-start = ((), (), s32[]{:S(2)}) async-start(), calls=%async_computation.2 | async-start | bytes 8388608 | tf_op jit(solution)/shard_map/psum | solution.py:18
  44.5 76.4 %copy-start = (f32[512,1024]{1,0:T(8,128)S(1)}, f32[512,1024]{1,0:T(8,128)}, u32[]{:S(2)}) copy-start(f32[512,1024]{1,0:T(8,128)} %all-gather.3.cloned.1.call-done) | copy-start | bytes 6291460
  110.9 10.0 %copy-start.3 = (f32[1024,512]{1,0:T(8,128)S(1)}, f32[1024,512]{1,0:T(8,128)}, u32[]{:S(2)}) copy-start(f32[1024,512]{1,0:T(8,128)} %param.4) | copy-start | bytes 6291460
  120.9 6.9 %copy-start.1 = (f32[1024,1024]{1,0:T(8,128)S(1)}, f32[1024,1024]{1,0:T(8,128)}, u32[]{:S(2)}) copy-start(f32[1024,1024]{1,0:T(8,128)} %all-gather.5.cloned.1.call-done) | copy-start | bytes 12582916
  283.5 15.6 %copy-start.2 = (f32[1024,1024]{1,0:T(8,128)S(1)}, f32[1024,1024]{1,0:T(8,128)}, u32[]{:S(2)}) copy-start(f32[1024,1024]{1,0:T(8,128)} %all-gather.5.cloned.1.call-done) | copy-start | bytes 12582916
Sparse Core Ops, SparseCore 0:
  8.9 25.2 all-gather.2
  36.2 74.6 all-gather.4
  142.9 140.6 all-reduce.1
where the time goes:
time: 389 us; the launch traced here: 383 us
  waiting for transfers between devices  235 us (60%)
  matrix products  72 us (19%)
  blocking collectives  39.5 us (10%)
  between operations  15 us (4%)
  other arithmetic  10.8 us (3%)
  local copies, waits for them, and re-layouts  10.7 us (3%)
    psum x1, waiting for transfers between devices, shards(): gradient = lax.psum(local_term, ('rows', 'cols'))  141 us
    dot_general x6, matrix products, product(): jnp.dot(left, right, precision=lax.Precision.HIGHEST, preferred_element_t...  72 us
    all_gather x1, waiting for transfers between devices, shards(): left_rows = lax.all_gather(left_factor, 'cols', axis=1, tiled=True)  66.5 us
    psum x1, blocking collectives, shards(): denom = lax.psum(jnp.sum(image * image), ('rows', 'cols'))  39.5 us
    all_gather x1, waiting for transfers between devices, shards(): right_rows = lax.all_gather(right_factor, 'rows', axis=1, tiled=True)  26.2 us
  transfers between devices with their start and end apart: 3, of which 3 were waited for; matrix products, arithmetic and copies ran while one was open for 3% of the time, Pallas kernels for 0%

commit v1 on v0

--- a/solution.py
+++ b/solution.py
@@ -10,7 +10,12 @@
 
 def shards(pair_integrals, left_factor, core, right_factor):
     left_rows = lax.all_gather(left_factor, "cols", axis=1, tiled=True)
-    right_rows = lax.all_gather(right_factor, "rows", axis=1, tiled=True)
+    ring = [right_factor]
+    for hop in range(3):
+        ring.append(lax.ppermute(ring[-1], "rows", [(dev, (dev + 1) % 4) for dev in range(4)]))
+    right_rows = jnp.roll(
+        jnp.concatenate(ring[::-1], axis=1), (lax.axis_index("rows") + 1) * ring[0].shape[1], axis=1
+    )
     mixed = product(core, right_rows.T)
     residual = pair_integrals - product(left_rows, mixed)
     along = product(residual, right_rows)

time: 389 us -> 365 us (0.938)
  waiting for transfers between devices: 235 us -> 210 us
    ppermute x0 -> x3, waiting for transfers between devices: none -> 26.2 us  [shards(): lax.ppermute(ring[-1], 'rows', [(dev, (dev + 1) % 4) for dev in range(4)])]
    all_gather x1 -> x0, waiting for transfers between devices: 26.2 us -> none  [shards(): right_rows = lax.all_gather(right_factor, 'rows', axis=1, tiled=True)]
    all_gather x1, waiting for transfers between devices: 66.5 us -> 42.1 us  [shards(): left_rows = lax.all_gather(left_factor, 'cols', axis=1, tiled=True)]
    unnamed x9 -> x22, local copies, waits for them, and re-layouts: 5.35 us -> 8.9 us
  transfers between devices with their start and end apart: 3 -> 5, of which waited for: 3 -> 5; matrix products, arithmetic and copies ran while one was open for 3% -> 2% of each run, Pallas kernels for 0% -> 0%
where the time goes in v1:
time: 365 us; the launch traced here: 359 us
  waiting for transfers between devices  210 us (58%)
  matrix products  68.6 us (19%)
  blocking collectives  39.5 us (11%)
  between operations  15.3 us (4%)
  local copies, waits for them, and re-layouts  14.3 us (4%)
  other arithmetic  10.8 us (3%)
    psum x1, waiting for transfers between devices, shards(): gradient = lax.psum(local_term, ('rows', 'cols'))  141 us
    dot_general x6, matrix products, product(): jnp.dot(left, right, precision=lax.Precision.HIGHEST, preferred_element_t...  68.6 us
    all_gather x1, waiting for transfers between devices, shards(): left_rows = lax.all_gather(left_factor, 'cols', axis=1, tiled=True)  42.1 us
    psum x1, blocking collectives, shards(): denom = lax.psum(jnp.sum(image * image), ('rows', 'cols'))  39.5 us
    ppermute x3, waiting for transfers between devices, shards(): lax.ppermute(ring[-1], 'rows', [(dev, (dev + 1) % 4) for dev in range(4)])  26.2 us
    unnamed x22, local copies, waits for them, and re-layouts  8.9 us
  transfers between devices with their start and end apart: 5, of which 5 were waited for; matrix products, arithmetic and copies ran while one was open for 2% of the time, Pallas kernels for 0%

profile of v1, /device:TPU:0, one launch (start us, length us, event | category | flops | bytes accessed | tf_op | source)
XLA Modules:
  0.0 359.0 jit_solution(8558803927966363968)
XLA Ops:
  6.5 0.0 copy-start.6
  6.5 0.0 all-gather.2.cloned.1.call-start
  6.5 0.7 all-gather.2.cloned.1.call-update
  7.3 0.0 all-reduce.2.cloned.1.call-start
  7.3 0.5 collective-permute-start
  7.8 9.0 %collective-permute-done = f32[512,256]{1,0:T(8,128)S(1)} collective-permute-done((f32[512,256]{1,0:T(8,128)}, f32[512,256]{1,0:T(8,128)S(1)}, u32[]{:S(2)}, u32[]{:S(2)}) %collective-permute-start) | collective-permute-done | bytes 524320 | tf_op jit(solution)/shard_map/ppermute | solution.py:15
  16.8 0.0 collective-permute-start.1
  16.9 8.6 %collective-permute-done.1 = f32[512,256]{1,0:T(8,128)S(1)} collective-permute-done((f32[512,256]{1,0:T(8,128)S(1)}, f32[512,256]{1,0:T(8,128)S(1)}, u32[]{:S(2)}, u32[]{:S(2)}) %collective-permute-start.1) | collective-permute-done | bytes 524320 | tf_op jit(solution)/shard_map/ppermute | solution.py:15
  25.4 0.0 collective-permute-start.2
  25.5 0.0 copy-start
  25.5 8.6 %collective-permute-done.2 = f32[512,256]{1,0:T(8,128)S(1)} collective-permute-done((f32[512,256]{1,0:T(8,128)S(1)}, f32[512,256]{1,0:T(8,128)S(1)}, u32[]{:S(2)}, u32[]{:S(2)}) %collective-permute-start.2) | collective-permute-done | bytes 524320 | tf_op jit(solution)/shard_map/ppermute | solution.py:15
  34.1 0.1 constant_dynamic-update-slice_fusion.7
  34.1 0.1 constant_dynamic-update-slice_fusion.6
  34.2 0.1 constant_dynamic-update-slice_fusion.5
  34.3 1.1 constant_dynamic-update-slice_fusion.4
  35.4 0.1 constant_dynamic-update-slice_fusion.3
  35.5 0.1 constant_dynamic-update-slice_fusion.2
  35.6 0.1 constant_dynamic-update-slice_fusion.1
  35.6 0.0 copy-done.6
  35.6 0.1 constant_dynamic-update-slice_fusion
  35.7 0.0 copy-start.1
  35.7 2.0 copy-done.1
  37.7 0.0 copy-done
  37.7 7.0 %fusion.4 = f32[512,1024]{1,0:T(8,128)S(1)} fusion(f32[1024,1024]{1,0:T(8,128)S(1)} %copy-done, f32[512,2048]{1,0:T(8,128)S(1)} %constant_dynamic-update-slice_fusion, s32[]{:T(128)S(6)} %select_n.14), kind=kOutput, calls=%fused_computation.9 | convolution fusion | flops 6442450944 | bytes 8388612 | tf_op jit(solution)/shard_map/dot_general | solution.py:8
  44.7 42.1 %all-gather.2.cloned.1.call-done = f32[1024,1024]{1,0:T(8,128)} async-done(((f32[1024,128]{1,0:T(8,128)}), f32[1024,1024]{1,0:T(8,128)}) %all-gather.2.cloned.1.call-update) | async-done | bytes 4194320 | tf_op jit(solution)/shard_map/all_gather | solution.py:12
  86.8 0.0 copy-start.2
  86.8 0.0 copy-start.3
  86.8 9.4 %fusion.9 = f32[512,1024]{0,1:T(8,128)S(1)} fusion(f32[512,1024]{1,0:T(8,128)S(1)} %fusion.4, f32[1024,1024]{1,0:T(8,128)} %all-gather.2.cloned.1.call-done), kind=kOutput, calls=%fused_computation.22 | convolution fusion | flops 6442450944 | bytes 8388608 | tf_op jit(solution)/shard_map/dot_general | solution.py:8
  96.2 0.0 copy-done.2
  96.2 0.0 copy-done.3
  96.2 0.0 copy-start.4
  96.2 6.9 %fusion = f32[1024,1024]{1,0:T(8,128)S(1)} fusion(f32[1024,512]{1,0:T(8,128)S(1)} %copy-done.3, f32[512,1024]{0,1:T(8,128)S(1)} %fusion.9, f32[512,2048]{1,0:T(8,128)S(1)} %copy-done.2, s32[]{:T(128)S(6)} %select_n.14), kind=kOutput, calls=%fused_computation.4 | convolution fusion | flops 6442975232 | bytes 10485764 | tf_op jit(solution)/shard_map/dot_general | solution.py:8
  103.1 0.0 copy-done.4
  103.1 15.0 %convolution_bitcast_fusion = f32[1024,1024]{0,1:T(8,128)} fusion(f32[1024,1024]{1,0:T(8,128)S(1)} %fusion, f32[1024,1024]{1,0:T(8,128)S(1)} %copy-done.4), kind=kOutput, calls=%fused_computation.2 | convolution fusion | flops 12884901888 | bytes 12582912 | tf_op jit(solution)/shard_map/dot_general | solution.py:8
  118.1 0.0 all-reduce.2.cloned.1.call-update
  118.1 140.9 %all-reduce.2.cloned.1.call-done = f32[1024,1024]{0,1:T(8,128)} async-done(((f32[1024,1024]{0,1:T(8,128)}), f32[1024,1024]{0,1:T(8,128)}) %all-reduce.2.cloned.1.call-update) | async-done | bytes 4194320 | tf_op jit(solution)/shard_map/psum | solution.py:23
  259.0 0.0 copy-start.5
  259.0 16.0 %fusion.1 = f32[1024,512]{1,0:T(8,128)S(1)} fusion(f32[1024,1024]{0,1:T(8,128)} %all-reduce.2.cloned.1.call-done, f32[512,2048]{1,0:T(8,128)} %copy-done.1, s32[]{:T(128)S(6)} %select_n.14), kind=kOutput, calls=%fused_computation.6 | convolution fusion | flops 6442450944 | bytes 8388612 | tf_op jit(solution)/shard_map/dot_general | solution.py:8
  275.0 0.0 copy-done.5
  275.1 14.3 %multiply_reduce_fusion.1 = f32[]{:T(128)} fusion(f32[1024,512]{1,0:T(8,128)S(1)} %fusion.1, f32[1024,1024]{1,0:T(8,128)S(1)} %copy-done.5), kind=kOutput, calls=%fused_computation.5 | convolution fusion | flops 6443499520 | bytes 6291460 | tf_op jit(solution)/shard_map/dot_general | solution.py:8
  289.4 5.3 %copy.5 = f32[1024,1024]{0,1:T(8,128)} copy(f32[1024,1024]{1,0:T(8,128)} %param.6) | data formatting | bytes 8388608 | tf_op args[2]
  294.7 39.5 %psum.15 = f32[]{:T(128)} all-reduce(f32[]{:T(128)} %multiply_reduce_fusion.1), channel_id=1, replica_groups=mesh['rows'=4,'cols'=8] {'rows','cols'}, use_global_device_ids=true, to_apply=%region_3.4 | all-reduce | flops 1 | bytes 8 | tf_op jit(solution)/shard_map/psum | solution.py:26
  334.2 3.9 %multiply_reduce_fusion = f32[]{:T(128)} fusion(f32[1024,1024]{0,1:T(8,128)} %all-reduce.2.cloned.1.call-done), kind=kLoop, calls=%fused_computation.1 | loop fusion | flops 2097151 | bytes 4194308 | tf_op jit(solution)/shard_map/reduce_sum | solution.py:24
  339.5 6.9 %multiply_add_fusion = f32[1024,1024]{0,1:T(8,128)} fusion(f32[1024,1024]{0,1:T(8,128)} %copy.5, f32[1024,1024]{0,1:T(8,128)} %all-reduce.2.cloned.1.call-done, f32[]{:T(128)S(6)} %div.3), kind=kLoop, calls=%fused_computation | loop fusion | flops 2097152 | bytes 12582916 | tf_op jit(solution)/shard_map/add | solution.py:27
  346.4 5.3 %copy.6 = f32[1024,1024]{1,0:T(8,128)} copy(f32[1024,1024]{0,1:T(8,128)} %multiply_add_fusion) | data formatting | bytes 8388608 | tf_op jit(solution)/shard_map/add | solution.py:27
Async XLA Ops:
  6.5 29.1 %copy-start.6 = (f32[512,256]{1,0:T(8,128)S(1)}, f32[512,256]{1,0:T(8,128)}, u32[]{:S(2)}) copy-start(f32[512,256]{1,0:T(8,128)} %param.7) | copy-start | bytes 1572868
  6.5 80.2 %all-gather.2.cloned.1.call-start = ((), (), s32[]{:S(2)}) async-start(), calls=%async_computation | async-start | bytes 4718592 | tf_op jit(solution)/shard_map/all_gather | solution.py:12
  7.3 251.7 %all-reduce.2.cloned.1.call-start = ((), (), s32[]{:S(2)}) async-start(), calls=%async_computation.1 | async-start | bytes 8388608 | tf_op jit(solution)/shard_map/psum | solution.py:23
  7.3 9.5 %collective-permute-start = (f32[512,256]{1,0:T(8,128)}, f32[512,256]{1,0:T(8,128)S(1)}, u32[]{:S(2)}, u32[]{:S(2)}) collective-permute-start(f32[512,256]{1,0:T(8,128)} %param.7), channel_id=1, source_target_pairs={{0,8},{8,16},{16,24},{24,0},{1,9},{9,17},{17,25},{25,1},{2,10},{10... | collective-permute-start | bytes 1572872 | tf_op jit(solution)/shard_map/ppermute | solution.py:15
  16.8 8.6 %collective-permute-start.1 = (f32[512,256]{1,0:T(8,128)S(1)}, f32[512,256]{1,0:T(8,128)S(1)}, u32[]{:S(2)}, u32[]{:S(2)}) collective-permute-start(f32[512,256]{1,0:T(8,128)S(1)} %collective-permute-done), channel_id=1, source_target_pairs={{0,8},{8,16},{16,24},{24,0},{1,9},{9,17},{17,25},{25,1},{2,10},{10... | collective-permute-start | bytes 1572872 | tf_op jit(solution)/shard_map/ppermute | solution.py:15
  25.4 8.6 %collective-permute-start.2 = (f32[512,256]{1,0:T(8,128)S(1)}, f32[512,256]{1,0:T(8,128)S(1)}, u32[]{:S(2)}, u32[]{:S(2)}) collective-permute-start(f32[512,256]{1,0:T(8,128)S(1)} %collective-permute-done.1), channel_id=1, source_target_pairs={{0,8},{8,16},{16,24},{24,0},{1,9},{9,17},{17,25},{25,1},{2,10},{10... | collective-permute-start | bytes 1572872 | tf_op jit(solution)/shard_map/ppermute | solution.py:15
  25.5 12.3 %copy-start = (f32[1024,1024]{1,0:T(8,128)S(1)}, f32[1024,1024]{1,0:T(8,128)}, u32[]{:S(2)}) copy-start(f32[1024,1024]{1,0:T(8,128)} %param.6) | copy-start | bytes 12582916
  35.7 2.0 copy-start.1
  86.8 9.4 %copy-start.2 = (f32[512,2048]{1,0:T(8,128)S(1)}, f32[512,2048]{1,0:T(8,128)}, u32[]{:S(2)}) copy-start(f32[512,2048]{1,0:T(8,128)} %copy-done.1) | copy-start | bytes 12582916
  86.8 9.4 %copy-start.3 = (f32[1024,512]{1,0:T(8,128)S(1)}, f32[1024,512]{1,0:T(8,128)}, u32[]{:S(2)}) copy-start(f32[1024,512]{1,0:T(8,128)} %param.4) | copy-start | bytes 6291460
  96.2 6.9 %copy-start.4 = (f32[1024,1024]{1,0:T(8,128)S(1)}, f32[1024,1024]{1,0:T(8,128)}, u32[]{:S(2)}) copy-start(f32[1024,1024]{1,0:T(8,128)} %all-gather.2.cloned.1.call-done) | copy-start | bytes 12582916
  259.0 16.0 %copy-start.5 = (f32[1024,1024]{1,0:T(8,128)S(1)}, f32[1024,1024]{1,0:T(8,128)}, u32[]{:S(2)}) copy-start(f32[1024,1024]{1,0:T(8,128)} %all-gather.2.cloned.1.call-done) | copy-start | bytes 12582916
Sparse Core Ops, SparseCore 0:
  9.4 77.3 all-gather.1
  118.3 140.6 all-reduce.1
